TPU v7x, 512 devices: a whole 4x8x8 slice. The times are simulated.
512 devices in a mesh: seq: 64 (over z, y_lo, core), head: 8 (over y_hi, x).
Axes of the slice: x: 4, y: 8 (y_hi: 2, y_lo: 4; y = y_hi * 4 + y_lo), z: 8, core: 2. Of those that a mesh axis runs over, the one named last changes fastest.
Arguments:
- query_in: bfloat16 [24576, 2048], P('seq', 'head'), may hold values from -6 to 6
- key_in: bfloat16 [24576, 2048], P('seq', 'head'), may hold values from -6 to 6
- value_in: bfloat16 [24576, 2048], P('seq', 'head'), may hold values from -6 to 6
- text_keys: bfloat16 [256, 2048], P(None, 'head'), may hold values from -6 to 6
- text_values: bfloat16 [256, 2048], P(None, 'head'), may hold values from -6 to 6
- text_mask: int32 [256], replicated, may hold values 0 or 1
- window_reach: int32 [16, 2], P('head'), may hold values from 0 to 1
- tile_map: int32 [64, 3], replicated, may hold values from 0 to 14, as said below
- out_weight: bfloat16 [2048, 3072], P('head'), may hold values from -0.125 to 0.125
- gate_scale: float32 [3072], replicated, may hold values from -4 to 4
- grad_out: bfloat16 [24576, 3072], P('seq', 'head'), may hold values from -12 to 12
Outputs:
- grad_query: bfloat16 [24576, 2048], P('seq', 'head')
- grad_key: bfloat16 [24576, 2048], P('seq', 'head')
- grad_value: bfloat16 [24576, 2048], P('seq', 'head')
- grad_text_keys: bfloat16 [256, 2048], P(None, 'head')
- grad_text_values: bfloat16 [256, 2048], P(None, 'head')
- grad_gate: float32 [3072], replicated
Inputs may be any that keep to these rules, and one draw needn't show every extreme that they name: `tile_map`: index i of seq sits at grid row i // 8 and grid column i % 8. Its tile row is that grid row, or 7 minus it, plus an offset; its tile column is the grid column, or 7 minus it, plus an offset; the mirroring and the offsets are the same for all indices, and so is the frame coordinate. Of the two offsets, the one of the longer grid dimension (rows when they are equal) is 7, the other 0.
All inputs are finite; a program needn't handle non-finite values.
Results may differ from a plain program's by a relative error of at most 0.02035.
The roundings to bfloat16 on the way count: a program that leaves them out, or rounds other values in their place, can miss the bound.
Values may be sent and summed in bfloat16 or wider, within the bound.
No kernel may reach another device: no remote copies, remote signals or barrier semaphores. Data moves between devices by JAX's collectives and lax.ppermute only.
A program may use at most 64 MiB of HBM per device.

v0:
```python
import jax
import jax.numpy as jnp
import numpy as np
from jax import lax
from jax.sharding import PartitionSpec as P

HEAD_DIM = 128
TILE_T = 6
TILE_H = 8
TILE_W = 8
COLS = 8
theta_base = 256.0


def from_behind(array, axis, by):
    length = lax.axis_size(axis)
    pairs = [(i, i + by) for i in range(length) if 0 <= i + by < length]
    return lax.ppermute(array, axis, pairs)


def sections(head_dim):
    first = head_dim // 8
    second = (head_dim - first) // 2
    return ((0, first), (first, second), (first + second, second))


def rotate(values, frame_pos, row_pos, col_pos, direction):
    pieces = []
    for (offset, length), where_pos in zip(
        sections(values.shape[-1]), (frame_pos, row_pos, col_pos)
    ):
        half_len = length // 2
        freqs = theta_base ** (-2.0 * jnp.arange(half_len, dtype=jnp.float32) / length)
        angles = where_pos.astype(jnp.float32)[:, None] * freqs[None, :]
        cosine = jnp.cos(angles)[:, None, :]
        sine_part = jnp.sin(angles)[:, None, :]
        first_half = values[..., offset : offset + half_len]
        second_half = values[..., offset + half_len : offset + length]
        pieces.append(first_half * cosine - direction * second_half * sine_part)
        pieces.append(direction * first_half * sine_part + second_half * cosine)
    return jnp.concatenate(pieces, axis=-1)


def local_positions(tile_coords):
    local_index = jnp.arange(TILE_T * TILE_H * TILE_W, dtype=jnp.int32)
    plane_size = TILE_H * TILE_W
    frame_pos = tile_coords[:, 0:1] * TILE_T + (local_index // plane_size)[None, :]
    row_pos = tile_coords[:, 1:2] * TILE_H + (local_index // TILE_W % TILE_H)[None, :]
    col_pos = tile_coords[:, 2:3] * TILE_W + (local_index % TILE_W)[None, :]
    return (frame_pos.reshape(-1), row_pos.reshape(-1), col_pos.reshape(-1))


def head_scores(queries, key_block, score_scale):
    return (
        jnp.einsum("qhd,khd->hqk", queries, key_block, preferred_element_type=jnp.float32)
        * score_scale
    )


def merge_stats(running_max, running_sum, scores):
    new_max = jnp.maximum(running_max, jnp.max(scores, axis=-1))
    new_sum = running_sum * jnp.exp(running_max - new_max) + jnp.sum(
        jnp.exp(scores - new_max[..., None]), axis=-1
    )
    return (new_max, new_sum)


def on_device(
    query_in,
    key_in,
    value_in,
    text_keys,
    text_values,
    text_mask,
    window_reach,
    tile_map,
    out_weight,
    gate_scale,
    grad_out,
):
    tile_rows = query_in.shape[0]
    feature_width = query_in.shape[1]
    head_count = feature_width // HEAD_DIM
    text_count = text_keys.shape[0]
    row_count = lax.axis_size("seq") // COLS
    device = lax.axis_index("seq")
    score_scale = HEAD_DIM ** (-0.5)
    split_shape = (tile_rows, head_count, HEAD_DIM)
    own_coords = tile_map[device]
    frame_pos, row_pos, col_pos = local_positions(own_coords[None, :])
    queries = rotate(
        query_in.astype(jnp.float32).reshape(split_shape), frame_pos, row_pos, col_pos, 1.0
    ).astype(jnp.bfloat16)
    keys_rot = rotate(
        key_in.astype(jnp.float32).reshape(split_shape), frame_pos, row_pos, col_pos, 1.0
    ).astype(jnp.bfloat16)
    packed = jnp.stack([keys_rot.reshape(tile_rows, feature_width), value_in])
    row_steps = np.array([-1, -1, -1, 0, 0, 0, 1, 1, 1], dtype=np.int32)
    col_steps = np.array([-1, 0, 1, -1, 0, 1, -1, 0, 1], dtype=np.int32)
    fetched = []
    for number in range(9):
        if number == 4:
            fetched.append(packed)
        else:
            fetched.append(
                from_behind(packed, "seq", int(row_steps[number]) * COLS + int(col_steps[number]))
            )
    blocks = jnp.stack(fetched)
    source_row = device // COLS - jnp.asarray(row_steps)
    source_col = device % COLS - jnp.asarray(col_steps)
    usable_block = (
        (source_row >= 0) & (source_row < row_count) & (source_col >= 0) & (source_col < COLS)
    )
    source = jnp.clip(source_row, 0, row_count - 1) * COLS + jnp.clip(source_col, 0, COLS - 1)
    near_coords = tile_map[source]
    row_gap = jnp.abs(near_coords[:, 1] - own_coords[1])
    col_gap = jnp.abs(near_coords[:, 2] - own_coords[2])
    allowed = (
        usable_block[None, :]
        & (row_gap[None, :] <= window_reach[:, 0:1])
        & (col_gap[None, :] <= window_reach[:, 1:2])
    )
    allow_rows = allowed.T
    text_open = (text_mask == 1)[None, None, :]
    block_keys = blocks[:, 0].reshape(9, tile_rows, head_count, HEAD_DIM)
    block_values = blocks[:, 1].reshape(9, tile_rows, head_count, HEAD_DIM)
    text_key_split = text_keys.reshape(text_count, head_count, HEAD_DIM)
    text_value_split = text_values.reshape(text_count, head_count, HEAD_DIM)

    def stats_step(carry, inputs):
        key_block, allow = inputs
        scores = jnp.where(
            allow[:, None, None], head_scores(queries, key_block, score_scale), -jnp.inf
        )
        return (merge_stats(carry[0], carry[1], scores), None)

    start_stats = (
        jnp.full((head_count, tile_rows), -1e30, jnp.float32),
        jnp.zeros((head_count, tile_rows), jnp.float32),
    )
    (running_max, running_sum), _ = lax.scan(stats_step, start_stats, (block_keys, allow_rows))
    text_scores = jnp.where(text_open, head_scores(queries, text_key_split, score_scale), -jnp.inf)
    running_max, running_sum = merge_stats(running_max, running_sum, text_scores)
    log_norm = running_max + jnp.log(running_sum)

    def weights_for(key_block, allow_mask):
        scores = head_scores(queries, key_block, score_scale)
        return jnp.where(allow_mask, jnp.exp(scores - log_norm[:, :, None]), 0.0)

    def output_step(total_out, inputs):
        key_block, value_block, allow = inputs
        probs = weights_for(key_block, allow[:, None, None]).astype(jnp.bfloat16)
        return (
            total_out
            + jnp.einsum("hqk,khd->hqd", probs, value_block, preferred_element_type=jnp.float32),
            None,
        )

    total_out, _ = lax.scan(
        output_step,
        jnp.zeros((head_count, tile_rows, HEAD_DIM), jnp.float32),
        (block_keys, block_values, allow_rows),
    )
    text_probs = weights_for(text_key_split, text_open).astype(jnp.bfloat16)
    total_out = total_out + jnp.einsum(
        "hqk,khd->hqd", text_probs, text_value_split, preferred_element_type=jnp.float32
    )
    attn = total_out.transpose(1, 0, 2).reshape(tile_rows, feature_width).astype(jnp.bfloat16)
    piece = lax.all_gather(grad_out, "head", axis=1, tiled=True)
    grad_proj = (piece.astype(jnp.float32) * gate_scale[None, :]).astype(jnp.bfloat16)
    grad_acc = lax.dot_general(
        grad_proj, out_weight, (((1,), (1,)), ((), ())), preferred_element_type=jnp.float32
    )
    projected = jnp.dot(attn, out_weight, preferred_element_type=jnp.float32)
    terms = jnp.sum(piece.astype(jnp.float32) * projected, axis=0)
    gate_terms = terms
    grad_attn, gate_terms = (grad_acc, gate_terms)
    grad_heads = grad_attn.astype(jnp.bfloat16).reshape(split_shape)
    delta = jnp.sum(
        grad_heads.astype(jnp.float32) * attn.reshape(split_shape).astype(jnp.float32), axis=-1
    ).T

    def grad_block(key_block, value_block, allow_mask):
        weights = weights_for(key_block, allow_mask)
        grad_weights = jnp.einsum(
            "qhd,khd->hqk", grad_heads, value_block, preferred_element_type=jnp.float32
        )
        grad_scores = (weights * (grad_weights - delta[:, :, None])).astype(jnp.bfloat16)
        query_part = jnp.einsum(
            "hqk,khd->hqd", grad_scores, key_block, preferred_element_type=jnp.float32
        )
        key_part = (
            jnp.einsum("hqk,qhd->khd", grad_scores, queries, preferred_element_type=jnp.float32)
            * score_scale
        )
        value_part = jnp.einsum(
            "hqk,qhd->khd",
            weights.astype(jnp.bfloat16),
            grad_heads,
            preferred_element_type=jnp.float32,
        )
        return (query_part, key_part, value_part)

    text_query_part, text_key_part, text_value_part = grad_block(
        text_key_split, text_value_split, text_open
    )
    text_key_grad = text_key_part.reshape(text_count, feature_width)
    text_value_grad = text_value_part.reshape(text_count, feature_width)

    def back_step(query_acc, inputs):
        key_block, value_block, allow = inputs
        query_part, key_part, value_part = grad_block(key_block, value_block, allow[:, None, None])
        stacked = jnp.stack(
            [
                key_part.reshape(tile_rows, feature_width),
                value_part.reshape(tile_rows, feature_width),
            ]
        )
        return (query_acc + query_part, stacked)

    query_acc, partials = lax.scan(
        back_step,
        jnp.zeros((head_count, tile_rows, HEAD_DIM), jnp.float32),
        (block_keys, block_values, allow_rows),
    )
    own_total = partials[4]
    for number in range(9):
        if number != 4:
            own_total = own_total + from_behind(
                partials[number].astype(jnp.bfloat16),
                "seq",
                -(int(row_steps[number]) * COLS + int(col_steps[number])),
            ).astype(jnp.float32)
    query_acc = query_acc + text_query_part
    text_key_sum, text_value_sum = lax.psum((text_key_grad, text_value_grad), "seq")
    grad_gate = lax.psum(gate_terms, ("seq", "head"))
    grad_query = (
        rotate((query_acc * score_scale).transpose(1, 0, 2), frame_pos, row_pos, col_pos, -1.0)
        .astype(jnp.bfloat16)
        .reshape(tile_rows, feature_width)
    )
    grad_key = (
        rotate(own_total[0].reshape(split_shape), frame_pos, row_pos, col_pos, -1.0)
        .astype(jnp.bfloat16)
        .reshape(tile_rows, feature_width)
    )
    grad_value = own_total[1].astype(jnp.bfloat16)
    return (
        grad_query,
        grad_key,
        grad_value,
        text_key_sum.astype(jnp.bfloat16),
        text_value_sum.astype(jnp.bfloat16),
        grad_gate,
    )


def solution(mesh):
    placed = (
        P("seq", "head"),
        P("seq", "head"),
        P("seq", "head"),
        P(None, "head"),
        P(None, "head"),
        P(),
        P("head", None),
        P(),
        P("head", None),
        P(),
        P("seq", "head"),
    )
    return jax.shard_map(
        on_device,
        mesh=mesh,
        in_specs=placed,
        out_specs=(
            P("seq", "head"),
            P("seq", "head"),
            P("seq", "head"),
            P(None, "head"),
            P(None, "head"),
            P(),
        ),
        check_vma=False,
    )
```

profile of v0, /device:TPU:2, one launch (start us, length us, event | category | flops | bytes accessed | tf_op | source)
XLA Modules:
  0.0 668.5 jit_solution(16040238661851726279)
XLA Ops:
  27.2 2.4 broadcast_multiply_fusion
  29.5 2.1 add_convert_fusion.8
  36.2 5.0 collective-permute-start.6
  41.2 5.4 collective-permute-start.5
  66.2 3.7 collective-permute-done
  74.5 15.0 %collective-permute-done.2 = bf16[2,384,256]{1,2,0:T(8,128)(2,1)S(1)} collective-permute-done((bf16[2,384,256]{1,2,0:T(8,128)(2,1)}, bf16[2,384,256]{1,2,0:T(8,128)(2,1)S(1)}, u32[]{:S(2)}, u32[]{:S(2)}) %collective-permute-start.2) | collective-permute-done | bytes 393248 | tf_op jit(solution)/shard_map/ppermute | solution.py:18
  96.5 2.3 fusion.93
  98.8 3.8 copy.126
  102.6 13.8 %while.37 = (s32[]{:T(128)}, f32[2,384]{1,0:T(2,128)S(1)}, f32[2,384]{1,0:T(2,128)S(1)}, pred[9,2]{1,0:T(8,128)(4,1)S(1)}, bf16[9,384,2,128]{3,1,2,0:T(8,128)(2,...) while((s32[]{:T(128)}, f32[2,384]{1,0:T(2,128)S(1)}, f32[2,384]{1,0:T(2,128)S(1)}, ...), condition=%wide.region_3.4_spmd.clone, body=%wide.region_0.3_spmd.clone.sunk | while | flops 76975872 | bytes 2792566 | solution.py:141
  117.0 3.9 copy.128
  121.2 29.6 %while.38 = (s32[]{:T(128)}, f32[2,384,128]{2,1,0:T(8,128)}, pred[9,2]{1,0:T(8,128)(4,1)}, bf16[9,384,2,128]{3,1,2,0:T(8,128)(2,1)}, bf16[384,2,128]{2,0,1:T(8,1...) while((s32[]{:T(128)}, f32[2,384,128]{2,1,0:T(8,128)}, ...), condition=%wide.region_7.8_spmd.clone, body=%wide.region_6.7_spmd.clone.sunk | while | flops 152371200 | bytes 1380984 | solution.py:159
  121.9 2.4 fusion.151
  125.0 2.6 fusion.151
  128.3 2.6 fusion.151
  131.6 2.6 fusion.151
  134.9 2.6 fusion.151
  138.2 2.6 fusion.151
  141.5 2.6 fusion.151
  144.8 2.6 fusion.151
  148.1 2.6 fusion.151
  152.7 2.7 fusion.53
  158.5 55.7 %while.39 = (s32[]{:T(128)}, f32[2,384,128]{2,1,0:T(8,128)S(1)}, f32[9,2,384,256]{2,3,1,0:T(8,128)}, pred[9,2]{1,0:T(8,128)(4,1)}, bf16[9,384,2,128]{3,1,2,0:T(8...) while((s32[]{:T(128)}, f32[2,384,128]{2,1,0:T(8,128)S(1)}, ...), condition=%wide.region_10.11_spmd.clone, body=%wide.region_9.10_spmd.clone.sunk | while | flops 380043264 | bytes 9836705 | solution.py:221
  214.2 3.6 convert.109
  219.5 5.7 collective-permute-start.8
  234.3 2.5 fusion.45
  236.9 126.0 %psum.23 = f32[3072]{0:T(1024)} all-reduce(f32[3072]{0:T(1024)S(1)} %fusion.45), channel_id=1, replica_groups=mesh['seq'=64,'head'=8] {'seq','head'}, use_global_device_ids=true, to_apply=%region_14.15 | all-reduce | flops 3072 | bytes 24576 | tf_op jit(solution)/shard_map/psum | solution.py:236
  362.9 2.5 collective-permute-start.11
  365.4 7.6 %collective-permute-start.10 = (bf16[2,384,256]{1,2,0:T(8,128)(2,1)}, bf16[2,384,256]{1,2,0:T(8,128)(2,1)}, u32[]{:S(2)}, u32[]{:S(2)}) collective-permute-start(bf16[2,384,256]{1,2,0:T(8,128)(2,1)} %get-tuple-element.347), channel_id=1, source_target_pairs={{0,56},{8,64},{16,72},{24,80},{32,88},{40,96},{48,104},{56,112},{6... | collective-permute-start | bytes 1179656 | tf_op jit(solution)/shard_map/ppermute | solution.py:18
  373.0 2.4 collective-permute-start.9
  375.7 269.2 %all-reduce.2 = (bf16[256,256]{1,0:T(8,128)(2,1)}, bf16[256,256]{1,0:T(8,128)(2,1)}) all-reduce(f32[256,256]{1,0:T(8,128)} %copy.146, f32[256,256]{1,0:T(8,128)S(1)} %copy.148), channel_id=1, replica_groups=mesh['seq'=64,'head'=8] {'seq'}, use_global_device_ids=true, to_apply=%region_11.12 | all-reduce | flops 131072 | bytes 786432 | tf_op jit(solution)/shard_map/psum | solution.py:235
  644.9 2.5 fusion.63
  653.8 2.2 add_convert_fusion.2
  (312 shorter events, 157.3 us)
Async XLA Ops:
  7.2 145.5 %copy-start = (bf16[256,3072]{1,0:T(8,128)(2,1)S(1)}, bf16[256,3072]{1,0:T(8,128)(2,1)}, u32[]{:S(2)}) copy-start(bf16[256,3072]{1,0:T(8,128)(2,1)} %param.27) | copy-start | bytes 4718596
  7.2 7.7 %copy-start.28 = (bf16[384,256]{1,0:T(8,128)(2,1)S(1)}, bf16[384,256]{1,0:T(8,128)(2,1)}, u32[]{:S(2)}) copy-start(bf16[384,256]{1,0:T(8,128)(2,1)} %param.21) | copy-start | bytes 589828
  7.2 145.5 %all-gather.2.cloned.1.call-start = ((), (), s32[]{:S(2)}) async-start(), calls=%async_computation | async-start | bytes 2654208 | tf_op jit(solution)/shard_map/all_gather | solution.py:169
  14.8 14.8 %copy-start.6 = (f32[384,8]{1,0:T(8,128)}, f32[384,8]{1,0:T(8,128)S(1)}, u32[]{:S(2)}) copy-start(f32[384,8]{1,0:T(8,128)S(1)} %copy.103) | copy-start | bytes 36868
  27.1 4.5 copy-start.12
  27.1 4.5 copy-start.13
  27.1 4.5 copy-start.14
  27.1 4.5 copy-start.15
  27.1 4.5 copy-start.16
  32.2 21.0 %copy-start.32 = (s32[2,2]{1,0:T(2,128)S(1)}, s32[2,2]{1,0:T(2,128)}, u32[]{:S(2)}) copy-start(s32[2,2]{1,0:T(2,128)} %param.25) | copy-start | bytes 52
  35.4 23.1 %copy-start.4 = (bf16[384,2,128]{0,2,1:T(8,128)(2,1)}, bf16[384,2,128]{0,2,1:T(8,128)(2,1)S(1)}, u32[]{:S(2)}) copy-start(bf16[384,2,128]{0,2,1:T(8,128)(2,1)S(1)} %copy.110) | copy-start | bytes 589828
  36.2 57.2 %collective-permute-start.6 = (bf16[2,384,256]{1,2,0:T(8,128)(2,1)}, bf16[2,384,256]{1,2,0:T(8,128)(2,1)}, u32[]{:S(2)}, u32[]{:S(2)}) collective-permute-start(bf16[2,384,256]{1,2,0:T(8,128)(2,1)} %pad_maximum_fusion), channel_id=1, source_target_pairs={{0,64},{8,72},{16,80},{24,88},{32,96},{40,104},{48,112},{56,120},{... | collective-permute-start | bytes 1179656 | tf_op jit(solution)/shard_map/ppermute | solution.py:18
  41.2 51.1 %collective-permute-start.5 = (bf16[2,384,256]{1,2,0:T(8,128)(2,1)}, bf16[2,384,256]{1,2,0:T(8,128)(2,1)}, u32[]{:S(2)}, u32[]{:S(2)}) collective-permute-start(bf16[2,384,256]{1,2,0:T(8,128)(2,1)} %pad_maximum_fusion), channel_id=1, source_target_pairs={{0,56},{8,64},{16,72},{24,80},{32,88},{40,96},{48,104},{56,112},{6... | collective-permute-start | bytes 1179656 | tf_op jit(solution)/shard_map/ppermute | solution.py:18
  46.7 44.6 %collective-permute-start.4 = (bf16[2,384,256]{1,2,0:T(8,128)(2,1)}, bf16[2,384,256]{1,2,0:T(8,128)(2,1)}, u32[]{:S(2)}, u32[]{:S(2)}) collective-permute-start(bf16[2,384,256]{1,2,0:T(8,128)(2,1)} %pad_maximum_fusion), channel_id=1, source_target_pairs={{0,8},{8,16},{16,24},{24,32},{32,40},{40,48},{48,56},{56,64},{64,7... | collective-permute-start | bytes 1179656 | tf_op jit(solution)/shard_map/ppermute | solution.py:18
  48.7 23.5 %collective-permute-start.1 = (bf16[2,384,256]{1,2,0:T(8,128)(2,1)}, bf16[2,384,256]{1,2,0:T(8,128)(2,1)}, u32[]{:S(2)}, u32[]{:S(2)}) collective-permute-start(bf16[2,384,256]{1,2,0:T(8,128)(2,1)} %pad_maximum_fusion), channel_id=1, source_target_pairs={{64,0},{72,8},{80,16},{88,24},{96,32},{104,40},{112,48},{120,56},{... | collective-permute-start | bytes 1179656 | tf_op jit(solution)/shard_map/ppermute | solution.py:18
  50.0 19.8 %collective-permute-start = (bf16[2,384,256]{1,2,0:T(8,128)(2,1)}, bf16[2,384,256]{1,2,0:T(8,128)(2,1)}, u32[]{:S(2)}, u32[]{:S(2)}) collective-permute-start(bf16[2,384,256]{1,2,0:T(8,128)(2,1)} %pad_maximum_fusion), channel_id=1, source_target_pairs={{72,0},{80,8},{88,16},{96,24},{104,32},{112,40},{120,48},{128,56},... | collective-permute-start | bytes 1179656 | tf_op jit(solution)/shard_map/ppermute | solution.py:18
  63.4 27.8 %copy-start.5 = (bf16[384,2,128]{0,2,1:T(8,128)(2,1)S(1)}, bf16[384,2,128]{0,2,1:T(8,128)(2,1)}, u32[]{:S(2)}) copy-start(bf16[384,2,128]{0,2,1:T(8,128)(2,1)} %copy-done.4) | copy-start | bytes 589828
  69.8 19.7 %collective-permute-start.2 = (bf16[2,384,256]{1,2,0:T(8,128)(2,1)}, bf16[2,384,256]{1,2,0:T(8,128)(2,1)S(1)}, u32[]{:S(2)}, u32[]{:S(2)}) collective-permute-start(bf16[2,384,256]{1,2,0:T(8,128)(2,1)} %pad_maximum_fusion), channel_id=1, source_target_pairs={{56,0},{64,8},{72,16},{80,24},{88,32},{96,40},{104,48},{112,56},{1... | collective-permute-start | bytes 1179656 | tf_op jit(solution)/shard_map/ppermute | solution.py:18
  72.2 19.0 %collective-permute-start.3 = (bf16[2,384,256]{1,2,0:T(8,128)(2,1)}, bf16[2,384,256]{1,2,0:T(8,128)(2,1)S(1)}, u32[]{:S(2)}, u32[]{:S(2)}) collective-permute-start(bf16[2,384,256]{1,2,0:T(8,128)(2,1)} %pad_maximum_fusion), channel_id=1, source_target_pairs={{8,0},{16,8},{24,16},{32,24},{40,32},{48,40},{56,48},{64,56},{72,6... | collective-permute-start | bytes 1179656 | tf_op jit(solution)/shard_map/ppermute | solution.py:18
  89.5 6.9 %collective-permute-start.7 = (bf16[2,384,256]{1,2,0:T(8,128)(2,1)}, bf16[2,384,256]{1,2,0:T(8,128)(2,1)S(1)}, u32[]{:S(2)}, u32[]{:S(2)}) collective-permute-start(bf16[2,384,256]{1,2,0:T(8,128)(2,1)} %pad_maximum_fusion), channel_id=1, source_target_pairs={{0,72},{8,80},{16,88},{24,96},{32,104},{40,112},{48,120},{56,128},... | collective-permute-start | bytes 1179656 | tf_op jit(solution)/shard_map/ppermute | solution.py:18
  217.7 10.1 %copy-start.1 = (bf16[2,384,256]{1,2,0:T(8,128)(2,1)S(1)}, bf16[2,384,256]{1,2,0:T(8,128)(2,1)}, u32[]{:S(2)}) copy-start(bf16[2,384,256]{1,2,0:T(8,128)(2,1)} %fusion.50) | copy-start | bytes 1179652
  219.5 14.8 %copy-start.27 = (bf16[2,384,128]{1,2,0:T(8,128)(2,1)S(1)}, bf16[2,384,128]{1,2,0:T(8,128)(2,1)}, u32[]{:S(2)}) copy-start(bf16[2,384,128]{1,2,0:T(8,128)(2,1)} %get-tuple-element.425) | copy-start | bytes 589828
  219.5 143.4 %collective-permute-start.8 = (bf16[2,384,256]{1,2,0:T(8,128)(2,1)}, bf16[2,384,256]{1,2,0:T(8,128)(2,1)}, u32[]{:S(2)}, u32[]{:S(2)}) collective-permute-start(bf16[2,384,256]{1,2,0:T(8,128)(2,1)} %get-tuple-element.341), channel_id=1, source_target_pairs={{0,72},{8,80},{16,88},{24,96},{32,104},{40,112},{48,120},{56,128},... | collective-permute-start | bytes 1179656 | tf_op jit(solution)/shard_map/ppermute | solution.py:18
  225.3 140.1 %collective-permute-start.15 = (bf16[2,384,256]{1,2,0:T(8,128)(2,1)}, bf16[2,384,256]{1,2,0:T(8,128)(2,1)}, u32[]{:S(2)}, u32[]{:S(2)}) collective-permute-start(bf16[2,384,256]{1,2,0:T(8,128)(2,1)} %get-tuple-element.342), channel_id=1, source_target_pairs={{72,0},{80,8},{88,16},{96,24},{104,32},{112,40},{120,48},{128,56},... | collective-permute-start | bytes 1179656 | tf_op jit(solution)/shard_map/ppermute | solution.py:18
  226.5 146.4 %collective-permute-start.14 = (bf16[2,384,256]{1,2,0:T(8,128)(2,1)}, bf16[2,384,256]{1,2,0:T(8,128)(2,1)}, u32[]{:S(2)}, u32[]{:S(2)}) collective-permute-start(bf16[2,384,256]{1,2,0:T(8,128)(2,1)} %get-tuple-element.343), channel_id=1, source_target_pairs={{64,0},{72,8},{80,16},{88,24},{96,32},{104,40},{112,48},{120,56},{... | collective-permute-start | bytes 1179656 | tf_op jit(solution)/shard_map/ppermute | solution.py:18
  231.7 413.2 %collective-permute-start.13 = (bf16[2,384,256]{1,2,0:T(8,128)(2,1)}, bf16[2,384,256]{1,2,0:T(8,128)(2,1)}, u32[]{:S(2)}, u32[]{:S(2)}) collective-permute-start(bf16[2,384,256]{1,2,0:T(8,128)(2,1)} %get-tuple-element.344), channel_id=1, source_target_pairs={{56,0},{64,8},{72,16},{80,24},{88,32},{96,40},{104,48},{112,56},{1... | collective-permute-start | bytes 1179656 | tf_op jit(solution)/shard_map/ppermute | solution.py:18
  233.0 411.9 %collective-permute-start.12 = (bf16[2,384,256]{1,2,0:T(8,128)(2,1)}, bf16[2,384,256]{1,2,0:T(8,128)(2,1)}, u32[]{:S(2)}, u32[]{:S(2)}) collective-permute-start(bf16[2,384,256]{1,2,0:T(8,128)(2,1)} %get-tuple-element.345), channel_id=1, source_target_pairs={{8,0},{16,8},{24,16},{32,24},{40,32},{48,40},{56,48},{64,56},{72,6... | collective-permute-start | bytes 1179656 | tf_op jit(solution)/shard_map/ppermute | solution.py:18
  234.3 141.0 %copy-start.21 = (bf16[256,256]{0,1:T(8,128)(2,1)S(1)}, bf16[256,256]{0,1:T(8,128)(2,1)}, u32[]{:S(2)}) copy-start(bf16[256,256]{0,1:T(8,128)(2,1)} %copy.182) | copy-start | bytes 393220
  362.9 282.0 %collective-permute-start.11 = (bf16[2,384,256]{1,2,0:T(8,128)(2,1)}, bf16[2,384,256]{1,2,0:T(8,128)(2,1)}, u32[]{:S(2)}, u32[]{:S(2)}) collective-permute-start(bf16[2,384,256]{1,2,0:T(8,128)(2,1)} %get-tuple-element.346), channel_id=1, source_target_pairs={{0,8},{8,16},{16,24},{24,32},{32,40},{40,48},{48,56},{56,64},{64,7... | collective-permute-start | bytes 1179656 | tf_op jit(solution)/shard_map/ppermute | solution.py:18
  365.4 279.6 %collective-permute-start.10 = (bf16[2,384,256]{1,2,0:T(8,128)(2,1)}, bf16[2,384,256]{1,2,0:T(8,128)(2,1)}, u32[]{:S(2)}, u32[]{:S(2)}) collective-permute-start(bf16[2,384,256]{1,2,0:T(8,128)(2,1)} %get-tuple-element.347), channel_id=1, source_target_pairs={{0,56},{8,64},{16,72},{24,80},{32,88},{40,96},{48,104},{56,112},{6... | collective-permute-start | bytes 1179656 | tf_op jit(solution)/shard_map/ppermute | solution.py:18
  373.0 272.0 %collective-permute-start.9 = (bf16[2,384,256]{1,2,0:T(8,128)(2,1)}, bf16[2,384,256]{1,2,0:T(8,128)(2,1)}, u32[]{:S(2)}, u32[]{:S(2)}) collective-permute-start(bf16[2,384,256]{1,2,0:T(8,128)(2,1)} %get-tuple-element.348), channel_id=1, source_target_pairs={{0,64},{8,72},{16,80},{24,88},{32,96},{40,104},{48,112},{56,120},{... | collective-permute-start | bytes 1179656 | tf_op jit(solution)/shard_map/ppermute | solution.py:18
  648.2 5.6 copy-start.7
  (19 other events, 61.0 us)
Sparse Core Ops, SparseCore 0:
  51.4 93.9 all-gather.1
where the time goes:
time: 672 us; the launch traced here: 668 us
  blocking collectives  395 us (59%)
  matrix products  86.9 us (13%)
  local copies, waits for them, and re-layouts  73.9 us (11%)
  starting transfers between devices  42.5 us (6%)
  other arithmetic  32 us (5%)
  waiting for transfers between devices  20.7 us (3%)
  between operations  16.5 us (2%)
    psum x1, blocking collectives, on_device(): lax.psum((text_key_grad, text_value_grad), 'seq')  269 us
    psum x1, blocking collectives, on_device(): grad_gate = lax.psum(gate_terms, ('seq', 'head'))  126 us
    ppermute x16, starting transfers between devices, from_behind(): return lax.ppermute(array, axis, pairs)  42.4 us
    unnamed x103, local copies, waits for them, and re-layouts  36.4 us
    dot_general x19, matrix products, head_scores(): jnp.einsum('qhd,khd->hqk', queries, key_block, preferred_element_type=jnp...  24.8 us
    dot_general x9, matrix products, output_step(): jnp.einsum('hqk,khd->hqd', probs, value_block, preferred_element_type=jnp...  23.4 us
    ppermute x16, waiting for transfers between devices, from_behind(): return lax.ppermute(array, axis, pairs)  20.7 us
  transfers between devices with their start and end apart: 17, of which 3 were waited for; matrix products, arithmetic and copies ran while one was open for 12% of the time, Pallas kernels for 0%

commit v1 on v0

--- a/solution.py
+++ b/solution.py
@@ -233,7 +233,7 @@
             ).astype(jnp.float32)
     query_acc = query_acc + text_query_part
     text_key_sum, text_value_sum = lax.psum((text_key_grad, text_value_grad), "seq")
-    grad_gate = lax.psum(gate_terms, ("seq", "head"))
+    grad_gate = lax.psum(lax.psum(gate_terms, "seq"), "head")
     grad_query = (
         rotate((query_acc * score_scale).transpose(1, 0, 2), frame_pos, row_pos, col_pos, -1.0)
         .astype(jnp.bfloat16)

time: 672 us -> 622 us (0.926)
  the two profiles are of different devices: /device:TPU:2 before, /device:TPU:256 now
where the time goes in v1:
time: 622 us; the launch traced here: 619 us
  blocking collectives  332 us (53%)
  matrix products  86.9 us (14%)
  local copies, waits for them, and re-layouts  68.3 us (11%)
  starting transfers between devices  60.9 us (10%)
  other arithmetic  33 us (5%)
  waiting for transfers between devices  20.1 us (3%)
  between operations  16.9 us (3%)
    psum x1, blocking collectives, on_device(): lax.psum((text_key_grad, text_value_grad), 'seq')  279 us
    ppermute x16, starting transfers between devices, from_behind(): return lax.ppermute(array, axis, pairs)  60.9 us
    psum x1, blocking collectives, on_device(): grad_gate = lax.psum(lax.psum(gate_terms, 'seq'), 'head')  53.6 us
    unnamed x111, local copies, waits for them, and re-layouts  33.3 us
    dot_general x19, matrix products, head_scores(): jnp.einsum('qhd,khd->hqk', queries, key_block, preferred_element_type=jnp...  24.7 us
    dot_general x9, matrix products, output_step(): jnp.einsum('hqk,khd->hqd', probs, value_block, preferred_element_type=jnp...  23.3 us
    ppermute x16, waiting for transfers between devices, from_behind(): return lax.ppermute(array, axis, pairs)  20.1 us
    dot_general x10, matrix products, grad_block(): jnp.einsum('hqk,khd->hqd', grad_scores, key_block, preferred_element_type...  12.5 us
  transfers between devices with their start and end apart: 17, of which 2 were waited for; matrix products, arithmetic and copies ran while one was open for 13% of the time, Pallas kernels for 0%

profile of v1, /device:TPU:256, one launch (start us, length us, event | category | flops | bytes accessed | tf_op | source)
XLA Modules:
  0.0 619.3 jit_solution(4183919905529003316)
XLA Ops:
  25.1 2.4 broadcast_multiply_fusion
  33.4 3.4 collective-permute-start.6
  36.8 4.7 collective-permute-start.5
  43.4 3.7 collective-permute-start.1
  47.0 5.8 collective-permute-start
  70.9 5.6 collective-permute-start.3
  77.6 5.5 collective-permute-done.2
  88.6 14.6 %collective-permute-done.7 = bf16[2,384,256]{1,2,0:T(8,128)(2,1)S(1)} collective-permute-done((bf16[2,384,256]{1,2,0:T(8,128)(2,1)}, bf16[2,384,256]{1,2,0:T(8,128)(2,1)S(1)}, u32[]{:S(2)}, u32[]{:S(2)}) %collective-permute-start.7) | collective-permute-done | bytes 393248 | tf_op jit(solution)/shard_map/ppermute | solution.py:18
  105.6 3.8 copy.126
  109.4 13.8 %while.37 = (s32[]{:T(128)}, f32[2,384]{1,0:T(2,128)S(1)}, f32[2,384]{1,0:T(2,128)S(1)}, pred[9,2]{1,0:T(8,128)(4,1)S(1)}, bf16[9,384,2,128]{3,1,2,0:T(8,128)(2,...) while((s32[]{:T(128)}, f32[2,384]{1,0:T(2,128)S(1)}, f32[2,384]{1,0:T(2,128)S(1)}, ...), condition=%wide.region_3.4_spmd.clone, body=%wide.region_0.3_spmd.clone.sunk | while | flops 76975872 | bytes 2792566 | solution.py:141
  123.8 3.9 copy.128
  127.9 29.5 %while.38 = (s32[]{:T(128)}, f32[2,384,128]{2,1,0:T(8,128)}, pred[9,2]{1,0:T(8,128)(4,1)}, bf16[9,384,2,128]{3,1,2,0:T(8,128)(2,1)}, bf16[384,2,128]{2,0,1:T(8,1...) while((s32[]{:T(128)}, f32[2,384,128]{2,1,0:T(8,128)}, ...), condition=%wide.region_7.8_spmd.clone, body=%wide.region_6.7_spmd.clone.sunk | while | flops 152371200 | bytes 1380984 | solution.py:159
  128.6 2.4 fusion.151
  131.7 2.6 fusion.151
  135.0 2.6 fusion.151
  138.3 2.6 fusion.151
  141.6 2.6 fusion.151
  144.9 2.6 fusion.151
  148.2 2.6 fusion.151
  151.5 2.6 fusion.151
  154.8 2.6 fusion.151
  159.4 2.7 fusion.53
  165.2 55.7 %while.39 = (s32[]{:T(128)}, f32[2,384,128]{2,1,0:T(8,128)S(1)}, f32[9,2,384,256]{2,3,1,0:T(8,128)}, pred[9,2]{1,0:T(8,128)(4,1)}, bf16[9,384,2,128]{3,1,2,0:T(8...) while((s32[]{:T(128)}, f32[2,384,128]{2,1,0:T(8,128)S(1)}, ...), condition=%wide.region_10.11_spmd.clone, body=%wide.region_9.10_spmd.clone.sunk | while | flops 380043264 | bytes 9836705 | solution.py:221
  220.8 3.6 convert.109
  228.1 8.4 %collective-permute-start.15 = (bf16[2,384,256]{1,2,0:T(8,128)(2,1)}, bf16[2,384,256]{1,2,0:T(8,128)(2,1)}, u32[]{:S(2)}, u32[]{:S(2)}) collective-permute-start(bf16[2,384,256]{1,2,0:T(8,128)(2,1)} %get-tuple-element.343), channel_id=1, source_target_pairs={{72,0},{80,8},{88,16},{96,24},{104,32},{112,40},{120,48},{128,56},... | collective-permute-start | bytes 1179656 | tf_op jit(solution)/shard_map/ppermute | solution.py:18
  242.7 3.8 collective-permute-start.12
  246.5 2.6 fusion.45
  251.1 7.9 %collective-permute-start.10 = (bf16[2,384,256]{1,2,0:T(8,128)(2,1)}, bf16[2,384,256]{1,2,0:T(8,128)(2,1)}, u32[]{:S(2)}, u32[]{:S(2)}) collective-permute-start(bf16[2,384,256]{1,2,0:T(8,128)(2,1)} %get-tuple-element.348), channel_id=1, source_target_pairs={{0,56},{8,64},{16,72},{24,80},{32,88},{40,96},{48,104},{56,112},{6... | collective-permute-start | bytes 1179656 | tf_op jit(solution)/shard_map/ppermute | solution.py:18
  259.1 3.9 collective-permute-start.9
  263.0 278.8 %all-reduce.2 = (bf16[256,256]{1,0:T(8,128)(2,1)}, bf16[256,256]{1,0:T(8,128)(2,1)}, f32[3072]{0:T(1024)S(1)}) all-reduce(f32[256,256]{1,0:T(8,128)S(1)} %copy.146, f32[256,256]{1,0:T(8,128)S(1)} %copy.148, f32[3072]{0:T(1024)S(1)} %fusion.45), channel_id=1, replica_groups=mesh['seq'=64,'head'=8] {'seq'}, use_global_device_ids=true, to_apply=%region_11.12 | all-reduce | flops 134144 | bytes 811008 | tf_op jit(solution)/shard_map/psum | solution.py:235
  541.8 53.6 %psum.31 = f32[3072]{0:T(1024)} all-reduce(f32[3072]{0:T(1024)S(1)} %get-tuple-element.339), channel_id=1, replica_groups=mesh['seq'=64,'head'=8] {'head'}, use_global_device_ids=true, to_apply=%region_15.16 | all-reduce | flops 3072 | bytes 24576 | tf_op jit(solution)/shard_map/psum | solution.py:236
  595.8 2.5 fusion.63
  (320 shorter events, 157.1 us)
Async XLA Ops:
  7.2 152.2 %copy-start = (bf16[256,3072]{1,0:T(8,128)(2,1)S(1)}, bf16[256,3072]{1,0:T(8,128)(2,1)}, u32[]{:S(2)}) copy-start(bf16[256,3072]{1,0:T(8,128)(2,1)} %param.27) | copy-start | bytes 4718596
  7.2 8.7 %copy-start.29 = (bf16[384,256]{1,0:T(8,128)(2,1)S(1)}, bf16[384,256]{1,0:T(8,128)(2,1)}, u32[]{:S(2)}) copy-start(bf16[384,256]{1,0:T(8,128)(2,1)} %param.21) | copy-start | bytes 589828
  7.2 152.1 %all-gather.2.cloned.1.call-start = ((), (), s32[]{:S(2)}) async-start(), calls=%async_computation | async-start | bytes 2654208 | tf_op jit(solution)/shard_map/all_gather | solution.py:169
  11.5 6.6 %copy-start.32 = (f32[384,2,8]{0,2,1:T(8,128)S(1)}, f32[384,2,8]{0,2,1:T(8,128)}, u32[]{:S(2)}) copy-start(f32[384,2,8]{0,2,1:T(8,128)} %get-tuple-element.400) | copy-start | bytes 73732
  11.5 6.8 %copy-start.28 = (f32[384,2,28]{0,2,1:T(8,128)S(1)}, f32[384,2,28]{0,2,1:T(8,128)}, u32[]{:S(2)}) copy-start(f32[384,2,28]{0,2,1:T(8,128)} %get-tuple-element.397) | copy-start | bytes 258052
  15.1 12.4 %copy-start.6 = (f32[384,8]{1,0:T(8,128)}, f32[384,8]{1,0:T(8,128)S(1)}, u32[]{:S(2)}) copy-start(f32[384,8]{1,0:T(8,128)S(1)} %copy.103) | copy-start | bytes 36868
  18.1 5.8 copy-start.30
  18.3 5.8 copy-start.31
  25.0 4.6 copy-start.13
  30.9 23.9 %copy-start.36 = (s32[2,2]{1,0:T(2,128)S(1)}, s32[2,2]{1,0:T(2,128)}, u32[]{:S(2)}) copy-start(s32[2,2]{1,0:T(2,128)} %param.25) | copy-start | bytes 52
  32.6 27.5 %copy-start.4 = (bf16[384,2,128]{0,2,1:T(8,128)(2,1)}, bf16[384,2,128]{0,2,1:T(8,128)(2,1)S(1)}, u32[]{:S(2)}) copy-start(bf16[384,2,128]{0,2,1:T(8,128)(2,1)S(1)} %copy.110) | copy-start | bytes 589828
  33.4 54.2 %collective-permute-start.6 = (bf16[2,384,256]{1,2,0:T(8,128)(2,1)}, bf16[2,384,256]{1,2,0:T(8,128)(2,1)}, u32[]{:S(2)}, u32[]{:S(2)}) collective-permute-start(bf16[2,384,256]{1,2,0:T(8,128)(2,1)} %pad_maximum_fusion), channel_id=1, source_target_pairs={{0,64},{8,72},{16,80},{24,88},{32,96},{40,104},{48,112},{56,120},{... | collective-permute-start | bytes 1179656 | tf_op jit(solution)/shard_map/ppermute | solution.py:18
  36.8 49.7 %collective-permute-start.5 = (bf16[2,384,256]{1,2,0:T(8,128)(2,1)}, bf16[2,384,256]{1,2,0:T(8,128)(2,1)}, u32[]{:S(2)}, u32[]{:S(2)}) collective-permute-start(bf16[2,384,256]{1,2,0:T(8,128)(2,1)} %pad_maximum_fusion), channel_id=1, source_target_pairs={{0,56},{8,64},{16,72},{24,80},{32,88},{40,96},{48,104},{56,112},{6... | collective-permute-start | bytes 1179656 | tf_op jit(solution)/shard_map/ppermute | solution.py:18
  41.4 44.0 %collective-permute-start.4 = (bf16[2,384,256]{1,2,0:T(8,128)(2,1)}, bf16[2,384,256]{1,2,0:T(8,128)(2,1)}, u32[]{:S(2)}, u32[]{:S(2)}) collective-permute-start(bf16[2,384,256]{1,2,0:T(8,128)(2,1)} %pad_maximum_fusion), channel_id=1, source_target_pairs={{0,8},{8,16},{16,24},{24,32},{32,40},{40,48},{48,56},{56,64},{64,7... | collective-permute-start | bytes 1179656 | tf_op jit(solution)/shard_map/ppermute | solution.py:18
  43.4 27.5 %collective-permute-start.1 = (bf16[2,384,256]{1,2,0:T(8,128)(2,1)}, bf16[2,384,256]{1,2,0:T(8,128)(2,1)}, u32[]{:S(2)}, u32[]{:S(2)}) collective-permute-start(bf16[2,384,256]{1,2,0:T(8,128)(2,1)} %pad_maximum_fusion), channel_id=1, source_target_pairs={{64,0},{72,8},{80,16},{88,24},{96,32},{104,40},{112,48},{120,56},{... | collective-permute-start | bytes 1179656 | tf_op jit(solution)/shard_map/ppermute | solution.py:18
  47.0 20.9 %collective-permute-start = (bf16[2,384,256]{1,2,0:T(8,128)(2,1)}, bf16[2,384,256]{1,2,0:T(8,128)(2,1)}, u32[]{:S(2)}, u32[]{:S(2)}) collective-permute-start(bf16[2,384,256]{1,2,0:T(8,128)(2,1)} %pad_maximum_fusion), channel_id=1, source_target_pairs={{72,0},{80,8},{88,16},{96,24},{104,32},{112,40},{120,48},{128,56},... | collective-permute-start | bytes 1179656 | tf_op jit(solution)/shard_map/ppermute | solution.py:18
  64.9 20.4 %copy-start.5 = (bf16[384,2,128]{0,2,1:T(8,128)(2,1)S(1)}, bf16[384,2,128]{0,2,1:T(8,128)(2,1)}, u32[]{:S(2)}) copy-start(bf16[384,2,128]{0,2,1:T(8,128)(2,1)} %copy-done.4) | copy-start | bytes 589828
  67.9 15.2 %collective-permute-start.2 = (bf16[2,384,256]{1,2,0:T(8,128)(2,1)}, bf16[2,384,256]{1,2,0:T(8,128)(2,1)S(1)}, u32[]{:S(2)}, u32[]{:S(2)}) collective-permute-start(bf16[2,384,256]{1,2,0:T(8,128)(2,1)} %pad_maximum_fusion), channel_id=1, source_target_pairs={{56,0},{64,8},{72,16},{80,24},{88,32},{96,40},{104,48},{112,56},{1... | collective-permute-start | bytes 1179656 | tf_op jit(solution)/shard_map/ppermute | solution.py:18
  70.9 14.3 %collective-permute-start.3 = (bf16[2,384,256]{1,2,0:T(8,128)(2,1)}, bf16[2,384,256]{1,2,0:T(8,128)(2,1)S(1)}, u32[]{:S(2)}, u32[]{:S(2)}) collective-permute-start(bf16[2,384,256]{1,2,0:T(8,128)(2,1)} %pad_maximum_fusion), channel_id=1, source_target_pairs={{8,0},{16,8},{24,16},{32,24},{40,32},{48,40},{56,48},{64,56},{72,6... | collective-permute-start | bytes 1179656 | tf_op jit(solution)/shard_map/ppermute | solution.py:18
  83.1 20.1 %collective-permute-start.7 = (bf16[2,384,256]{1,2,0:T(8,128)(2,1)}, bf16[2,384,256]{1,2,0:T(8,128)(2,1)S(1)}, u32[]{:S(2)}, u32[]{:S(2)}) collective-permute-start(bf16[2,384,256]{1,2,0:T(8,128)(2,1)} %pad_maximum_fusion), channel_id=1, source_target_pairs={{0,72},{8,80},{16,88},{24,96},{32,104},{40,112},{48,120},{56,128},... | collective-permute-start | bytes 1179656 | tf_op jit(solution)/shard_map/ppermute | solution.py:18
  224.4 14.1 %copy-start.1 = (bf16[2,384,256]{1,2,0:T(8,128)(2,1)S(1)}, bf16[2,384,256]{1,2,0:T(8,128)(2,1)}, u32[]{:S(2)}) copy-start(bf16[2,384,256]{1,2,0:T(8,128)(2,1)} %fusion.50) | copy-start | bytes 1179652
  224.4 15.1 %copy-start.22 = (f32[2,128,256]{2,1,0:T(8,128)S(1)}, f32[2,128,256]{2,1,0:T(8,128)}, u32[]{:S(2)}) copy-start(f32[2,128,256]{2,1,0:T(8,128)} %fusion.89) | copy-start | bytes 786436
  226.2 23.0 %collective-permute-start.8 = (bf16[2,384,256]{1,2,0:T(8,128)(2,1)}, bf16[2,384,256]{1,2,0:T(8,128)(2,1)}, u32[]{:S(2)}, u32[]{:S(2)}) collective-permute-start(bf16[2,384,256]{1,2,0:T(8,128)(2,1)} %get-tuple-element.342), channel_id=1, source_target_pairs={{0,72},{8,80},{16,88},{24,96},{32,104},{40,112},{48,120},{56,128},... | collective-permute-start | bytes 1179656 | tf_op jit(solution)/shard_map/ppermute | solution.py:18
  228.1 23.0 %collective-permute-start.15 = (bf16[2,384,256]{1,2,0:T(8,128)(2,1)}, bf16[2,384,256]{1,2,0:T(8,128)(2,1)}, u32[]{:S(2)}, u32[]{:S(2)}) collective-permute-start(bf16[2,384,256]{1,2,0:T(8,128)(2,1)} %get-tuple-element.343), channel_id=1, source_target_pairs={{72,0},{80,8},{88,16},{96,24},{104,32},{112,40},{120,48},{128,56},... | collective-permute-start | bytes 1179656 | tf_op jit(solution)/shard_map/ppermute | solution.py:18
  236.6 22.5 %collective-permute-start.14 = (bf16[2,384,256]{1,2,0:T(8,128)(2,1)}, bf16[2,384,256]{1,2,0:T(8,128)(2,1)}, u32[]{:S(2)}, u32[]{:S(2)}) collective-permute-start(bf16[2,384,256]{1,2,0:T(8,128)(2,1)} %get-tuple-element.344), channel_id=1, source_target_pairs={{64,0},{72,8},{80,16},{88,24},{96,32},{104,40},{112,48},{120,56},{... | collective-permute-start | bytes 1179656 | tf_op jit(solution)/shard_map/ppermute | solution.py:18
  240.7 355.0 %collective-permute-start.13 = (bf16[2,384,256]{1,2,0:T(8,128)(2,1)}, bf16[2,384,256]{1,2,0:T(8,128)(2,1)}, u32[]{:S(2)}, u32[]{:S(2)}) collective-permute-start(bf16[2,384,256]{1,2,0:T(8,128)(2,1)} %get-tuple-element.345), channel_id=1, source_target_pairs={{56,0},{64,8},{72,16},{80,24},{88,32},{96,40},{104,48},{112,56},{1... | collective-permute-start | bytes 1179656 | tf_op jit(solution)/shard_map/ppermute | solution.py:18
  242.7 353.1 %collective-permute-start.12 = (bf16[2,384,256]{1,2,0:T(8,128)(2,1)}, bf16[2,384,256]{1,2,0:T(8,128)(2,1)}, u32[]{:S(2)}, u32[]{:S(2)}) collective-permute-start(bf16[2,384,256]{1,2,0:T(8,128)(2,1)} %get-tuple-element.346), channel_id=1, source_target_pairs={{8,0},{16,8},{24,16},{32,24},{40,32},{48,40},{56,48},{64,56},{72,6... | collective-permute-start | bytes 1179656 | tf_op jit(solution)/shard_map/ppermute | solution.py:18
  246.5 348.9 %copy-start.21 = (bf16[256,256]{0,1:T(8,128)(2,1)S(1)}, bf16[256,256]{0,1:T(8,128)(2,1)}, u32[]{:S(2)}) copy-start(bf16[256,256]{0,1:T(8,128)(2,1)} %copy.182) | copy-start | bytes 393220
  249.2 346.6 %collective-permute-start.11 = (bf16[2,384,256]{1,2,0:T(8,128)(2,1)}, bf16[2,384,256]{1,2,0:T(8,128)(2,1)}, u32[]{:S(2)}, u32[]{:S(2)}) collective-permute-start(bf16[2,384,256]{1,2,0:T(8,128)(2,1)} %get-tuple-element.347), channel_id=1, source_target_pairs={{0,8},{8,16},{16,24},{24,32},{32,40},{40,48},{48,56},{56,64},{64,7... | collective-permute-start | bytes 1179656 | tf_op jit(solution)/shard_map/ppermute | solution.py:18
  251.1 344.7 %collective-permute-start.10 = (bf16[2,384,256]{1,2,0:T(8,128)(2,1)}, bf16[2,384,256]{1,2,0:T(8,128)(2,1)}, u32[]{:S(2)}, u32[]{:S(2)}) collective-permute-start(bf16[2,384,256]{1,2,0:T(8,128)(2,1)} %get-tuple-element.348), channel_id=1, source_target_pairs={{0,56},{8,64},{16,72},{24,80},{32,88},{40,96},{48,104},{56,112},{6... | collective-permute-start | bytes 1179656 | tf_op jit(solution)/shard_map/ppermute | solution.py:18
  259.1 336.7 %collective-permute-start.9 = (bf16[2,384,256]{1,2,0:T(8,128)(2,1)}, bf16[2,384,256]{1,2,0:T(8,128)(2,1)}, u32[]{:S(2)}, u32[]{:S(2)}) collective-permute-start(bf16[2,384,256]{1,2,0:T(8,128)(2,1)} %get-tuple-element.349), channel_id=1, source_target_pairs={{0,64},{8,72},{16,80},{24,88},{32,96},{40,104},{48,112},{56,120},{... | collective-permute-start | bytes 1179656 | tf_op jit(solution)/shard_map/ppermute | solution.py:18
  599.0 5.6 copy-start.7
  (23 other events, 80.3 us)
Sparse Core Ops, SparseCore 0:
  53.0 86.9 all-gather.1
